TPU v7x, 32 devices: a whole 2x2x4 slice. The times are simulated.
32 devices in a mesh: tm: 8 (over z, x), lon: 4 (over y, core).
Axes of the slice: x: 2, y: 2, z: 4, core: 2. Of those that a mesh axis runs over, the one named last changes fastest.
Arguments:
- start: float32 [3, 128, 512], P(None, 'lon'), may hold values from -6 to 6
- depth: float32 [128, 512], P('lon'), may hold values from 0.5 to 1.5
Outputs:
- ends: float32 [8, 3, 128, 512], P('tm', None, 'lon')
All inputs are finite; a program needn't handle non-finite values.
Results may differ from a plain program's by a relative error of at most 0.00002.
Values sent between devices are 32-bit elements; how exact they have to be, the bound alone decides.
No kernel may reach another device: no remote copies, remote signals or barrier semaphores. Data moves between devices by JAX's collectives and lax.ppermute only.
A program may use at most 64 MiB of HBM per device.

v0:
```python
import math
import jax
import jax.numpy as jnp
from jax import lax
from jax.sharding import PartitionSpec as P

STEPS = 3
ROUNDS = 2
LAT_LIMIT = 1.2
COURANT = 1.2
DEPTH_MAX = 1.5
GRAVITY = 1.0
TURN_RATE = 0.15


def padded_2(cells, sides, width):
    for axis, dim in sides:
        count = lax.axis_size(axis)
        head = lax.slice_in_dim(cells, 0, width, axis=dim)
        tail = lax.slice_in_dim(cells, cells.shape[dim] - width, cells.shape[dim], axis=dim)
        cells = jnp.concatenate(
            [
                lax.ppermute(tail, axis, [(i, (i + 1) % count) for i in range(count)]),
                cells,
                lax.ppermute(head, axis, [((i + 1) % count, i) for i in range(count)]),
            ],
            axis=dim,
        )
    return cells


def grid_constants(lon_cells, lat_cells):
    latitude = -LAT_LIMIT + (jnp.arange(lat_cells, dtype=jnp.float32) + 0.5) * (
        2.0 * LAT_LIMIT / lat_cells
    )
    cosine = jnp.cos(latitude)
    north_spacing = 2.0 * LAT_LIMIT / lat_cells
    east_spacing = cosine * (2.0 * math.pi / lon_cells)
    narrowest = math.cos(LAT_LIMIT - LAT_LIMIT / lat_cells) * 2.0 * math.pi / lon_cells
    time_step = COURANT / (
        math.sqrt(DEPTH_MAX * GRAVITY) * math.sqrt(1.0 / narrowest**2 + 1.0 / north_spacing**2)
    )
    coriolis = TURN_RATE * jnp.sin(latitude) / time_step
    turning = coriolis * (STEPS * time_step)
    return (cosine, east_spacing, north_spacing, time_step, coriolis, turning)


def north_diff(values):
    padded = jnp.pad(values, ((0, 0), (1, 1)))
    return padded[:, 2:] - padded[:, :-2]


def advance_split(state, depth, consts):
    cosine, east_spacing, north_spacing, time_step, coriolis, turning = consts
    height = state[0]
    zonal = state[1]
    merid = state[2]
    flux_wide = padded_2(depth * zonal, (("lon", 0),), 1)
    flux_north = depth * merid * cosine
    diverge = (flux_wide[2:] - flux_wide[:-2]) / (2.0 * east_spacing) + north_diff(flux_north) / (
        2.0 * north_spacing * cosine
    )
    height_new = height - time_step * diverge
    height_wide = padded_2(height_new, (("lon", 0),), 1)
    zonal_new = zonal + time_step * (
        coriolis * merid - GRAVITY * (height_wide[2:] - height_wide[:-2]) / (2.0 * east_spacing)
    )
    merid_new = merid + time_step * (
        -coriolis * zonal_new - GRAVITY * north_diff(height_new) / (2.0 * north_spacing)
    )
    return jnp.stack([height_new, zonal_new, merid_new])


def rotate(state, angle):
    cos_angle = jnp.cos(angle)
    sin_angle = jnp.sin(angle)
    zonal = state[..., 1, :, :]
    merid = state[..., 2, :, :]
    return jnp.stack(
        [
            state[..., 0, :, :],
            zonal * cos_angle + merid * sin_angle,
            merid * cos_angle - zonal * sin_angle,
        ],
        axis=-3,
    )


def body(start, depth):
    lon_cells = start.shape[1] * lax.axis_size("lon")
    lat_cells = start.shape[2]
    consts = grid_constants(lon_cells, lat_cells)
    turning = consts[5]
    number = lax.axis_index("tm").astype(jnp.float32)
    guess = rotate(start, number * turning)
    ends = guess
    for round_index in range(ROUNDS):
        state = guess
        for turn_index in range(STEPS):
            state = advance_split(state, depth, consts)
        correct = state - rotate(guess, turning)
        carried = rotate(correct, -(number + 1.0) * turning)
        stacked = lax.all_to_all(carried[None], "tm", split_axis=2, concat_axis=0, tiled=True)
        running = jnp.cumsum(stacked, axis=0)
        running = jnp.concatenate([jnp.zeros_like(stacked[:1]), running[:-1]], axis=0)
        before = lax.all_to_all(running, "tm", split_axis=0, concat_axis=2, tiled=True)[0]
        total = start + before
        if round_index + 1 < ROUNDS:
            guess = rotate(total, number * turning)
        else:
            ends = rotate(total + carried, (number + 1.0) * turning)
    return ends[None]


def solution(mesh):
    return jax.shard_map(
        body,
        mesh=mesh,
        in_specs=(P(None, "lon", None), P("lon", None)),
        out_specs=P("tm", None, "lon", None),
        check_vma=False,
    )
```

profile of v0, /device:TPU:0, one launch (start us, length us, event | category | flops | bytes accessed | tf_op | source)
XLA Modules:
  0.0 90.6 jit_solution(3166907388512287676)
XLA Ops:
  0.2 1.0 %multiply_multiply_fusion.5 = (f32[32,512]{1,0:T(8,128)S(1)}, f32[32,512]{1,0:T(8,128)S(1)}, f32[32,512]{1,0:T(8,128)S(1)}) fusion(f32[32,512]{1,0:T(8,128)} %param.3, f32[512]{0:T(512)S(1)} %fusion.117, f32[512]{0:T(512)S(1)} %get-tuple-element.70, f32[3,32,512]{2,1,0:T(8,128)} %param.2, f32[512]{0:T(512)S(1)} %get-tuple-element.71), kind=kLoop, calls=%fused_computation.196 | loop fusion | flops 147456 | bytes 399360 | tf_op jit(solution)/shard_map/mul | solution.py:59
  1.1 2.5 %collective-permute-start = (f32[1,512]{1,0:T(1,128)S(1)}, f32[1,512]{1,0:T(1,128)S(1)}, u32[]{:S(2)}, u32[]{:S(2)}) collective-permute-start(f32[1,512]{1,0:T(1,128)S(1)} %get-tuple-element.68), channel_id=1, source_target_pairs={{1,0},{2,1},{3,2},{0,3},{5,4},{6,5},{7,6},{4,7},{9,8},{10,9},{11,1... | collective-permute-start | bytes 6152 | tf_op jit(solution)/shard_map/ppermute | solution.py:25
  3.8 1.1 %collective-permute-done = f32[1,512]{1,0:T(1,128)S(1)} collective-permute-done((f32[1,512]{1,0:T(1,128)S(1)}, f32[1,512]{1,0:T(1,128)S(1)}, u32[]{:S(2)}, u32[]{:S(2)}) %collective-permute-start) | collective-permute-done | bytes 2080 | tf_op jit(solution)/shard_map/ppermute | solution.py:25
  4.9 1.7 %collective-permute-done.1 = f32[1,512]{1,0:T(1,128)S(1)} collective-permute-done((f32[1,512]{1,0:T(1,128)S(1)}, f32[1,512]{1,0:T(1,128)S(1)}, u32[]{:S(2)}, u32[]{:S(2)}) %collective-permute-start.1) | collective-permute-done | bytes 2080 | tf_op jit(solution)/shard_map/ppermute | solution.py:23
  7.4 0.8 collective-permute-done.2
  8.1 1.8 %collective-permute-done.3 = f32[1,512]{1,0:T(1,128)S(1)} collective-permute-done((f32[1,512]{1,0:T(1,128)S(1)}, f32[1,512]{1,0:T(1,128)S(1)}, u32[]{:S(2)}, u32[]{:S(2)}) %collective-permute-start.3) | collective-permute-done | bytes 2080 | tf_op jit(solution)/shard_map/ppermute | solution.py:23
  10.6 0.7 collective-permute-done.4
  11.3 1.8 %collective-permute-done.5 = f32[1,512]{1,0:T(1,128)S(1)} collective-permute-done((f32[1,512]{1,0:T(1,128)S(1)}, f32[1,512]{1,0:T(1,128)S(1)}, u32[]{:S(2)}, u32[]{:S(2)}) %collective-permute-start.5) | collective-permute-done | bytes 2080 | tf_op jit(solution)/shard_map/ppermute | solution.py:23
  13.8 0.8 collective-permute-done.6
  14.6 1.8 %collective-permute-done.7 = f32[1,512]{1,0:T(1,128)S(1)} collective-permute-done((f32[1,512]{1,0:T(1,128)S(1)}, f32[1,512]{1,0:T(1,128)S(1)}, u32[]{:S(2)}, u32[]{:S(2)}) %collective-permute-start.7) | collective-permute-done | bytes 2080 | tf_op jit(solution)/shard_map/ppermute | solution.py:23
  17.1 0.7 collective-permute-done.8
  17.8 1.8 %collective-permute-done.9 = f32[1,512]{1,0:T(1,128)S(1)} collective-permute-done((f32[1,512]{1,0:T(1,128)S(1)}, f32[1,512]{1,0:T(1,128)S(1)}, u32[]{:S(2)}, u32[]{:S(2)}) %collective-permute-start.9) | collective-permute-done | bytes 2080 | tf_op jit(solution)/shard_map/ppermute | solution.py:23
  20.3 0.7 collective-permute-done.10
  21.0 1.8 %collective-permute-done.11 = f32[1,512]{1,0:T(1,128)S(1)} collective-permute-done((f32[1,512]{1,0:T(1,128)S(1)}, f32[1,512]{1,0:T(1,128)S(1)}, u32[]{:S(2)}, u32[]{:S(2)}) %collective-permute-start.11) | collective-permute-done | bytes 2080 | tf_op jit(solution)/shard_map/ppermute | solution.py:23
  23.2 13.4 %all_to_all.66 = f32[1,3,32,512]{3,0,1,2:T(1,128)S(1)} all-to-all(f32[1,3,32,512]{3,0,1,2:T(1,128)S(1)} %copy.63), channel_id=1, replica_groups=mesh['tm'=8,'lon'=4] {'tm'}, dimensions={2} | all-to-all | bytes 393216 | tf_op jit(solution)/shard_map/all_to_all | solution.py:103
  36.8 10.2 %all_to_all.67 = f32[8,3,4,512]{3,2,1,0:T(4,128)S(1)} all-to-all(f32[8,3,4,512]{3,2,1,0:T(4,128)S(1)} %concatenate.102.clone), channel_id=1, replica_groups=mesh['tm'=8,'lon'=4] {'tm'}, dimensions={0} | all-to-all | bytes 393216 | tf_op jit(solution)/shard_map/all_to_all | solution.py:106
  47.7 0.8 collective-permute-done.12
  48.5 1.8 %collective-permute-done.13 = f32[1,512]{1,0:T(1,128)S(1)} collective-permute-done((f32[1,512]{1,0:T(1,128)S(1)}, f32[1,512]{1,0:T(1,128)S(1)}, u32[]{:S(2)}, u32[]{:S(2)}) %collective-permute-start.13) | collective-permute-done | bytes 2080 | tf_op jit(solution)/shard_map/ppermute | solution.py:23
  51.0 0.8 collective-permute-done.14
  51.8 1.8 %collective-permute-done.15 = f32[1,512]{1,0:T(1,128)S(1)} collective-permute-done((f32[1,512]{1,0:T(1,128)S(1)}, f32[1,512]{1,0:T(1,128)S(1)}, u32[]{:S(2)}, u32[]{:S(2)}) %collective-permute-start.15) | collective-permute-done | bytes 2080 | tf_op jit(solution)/shard_map/ppermute | solution.py:23
  54.3 0.7 collective-permute-done.16
  55.0 1.8 %collective-permute-done.17 = f32[1,512]{1,0:T(1,128)S(1)} collective-permute-done((f32[1,512]{1,0:T(1,128)S(1)}, f32[1,512]{1,0:T(1,128)S(1)}, u32[]{:S(2)}, u32[]{:S(2)}) %collective-permute-start.17) | collective-permute-done | bytes 2080 | tf_op jit(solution)/shard_map/ppermute | solution.py:23
  57.4 0.8 collective-permute-done.18
  58.2 1.8 %collective-permute-done.19 = f32[1,512]{1,0:T(1,128)S(1)} collective-permute-done((f32[1,512]{1,0:T(1,128)S(1)}, f32[1,512]{1,0:T(1,128)S(1)}, u32[]{:S(2)}, u32[]{:S(2)}) %collective-permute-start.19) | collective-permute-done | bytes 2080 | tf_op jit(solution)/shard_map/ppermute | solution.py:23
  60.7 0.7 collective-permute-done.20
  61.4 1.8 %collective-permute-done.21 = f32[1,512]{1,0:T(1,128)S(1)} collective-permute-done((f32[1,512]{1,0:T(1,128)S(1)}, f32[1,512]{1,0:T(1,128)S(1)}, u32[]{:S(2)}, u32[]{:S(2)}) %collective-permute-start.21) | collective-permute-done | bytes 2080 | tf_op jit(solution)/shard_map/ppermute | solution.py:23
  63.9 0.8 collective-permute-done.22
  64.7 1.8 %collective-permute-done.23 = f32[1,512]{1,0:T(1,128)S(1)} collective-permute-done((f32[1,512]{1,0:T(1,128)S(1)}, f32[1,512]{1,0:T(1,128)S(1)}, u32[]{:S(2)}, u32[]{:S(2)}) %collective-permute-start.23) | collective-permute-done | bytes 2080 | tf_op jit(solution)/shard_map/ppermute | solution.py:23
  66.8 10.9 %all_to_all.68 = f32[1,3,32,512]{3,0,1,2:T(1,128)S(1)} all-to-all(f32[1,3,32,512]{3,0,1,2:T(1,128)S(1)} %copy.67), channel_id=1, replica_groups=mesh['tm'=8,'lon'=4] {'tm'}, dimensions={2} | all-to-all | bytes 393216 | tf_op jit(solution)/shard_map/all_to_all | solution.py:103
  77.9 0.7 concatenate.115.clone
  78.6 3.4 %all-to-all-start.3 = ((f32[8,3,4,512]{3,2,1,0:T(4,128)}), f32[8,3,4,512]{3,2,1,0:T(4,128)S(1)}, u32[]{:S(2)}, u32[]{:S(2)}) async-start(f32[8,3,4,512]{3,2,1,0:T(4,128)} %concatenate.115.clone), calls=%async_computation.3 | async-start | bytes 393216 | tf_op jit(solution)/shard_map/all_to_all | solution.py:106
  82.1 7.6 %all-to-all-done.3 = f32[8,3,4,512]{3,2,1,0:T(4,128)S(1)} async-done(((f32[8,3,4,512]{3,2,1,0:T(4,128)}), f32[8,3,4,512]{3,2,1,0:T(4,128)S(1)}, u32[]{:S(2)}, u32[]{:S(2)}) %all-to-all-start.3) | async-done | bytes 196640 | tf_op jit(solution)/shard_map/all_to_all | solution.py:106
  (91 shorter events, 10.0 us)
Async XLA Ops:
  0.1 6.5 %copy-start.1 = (f32[3,32,512]{2,1,0:T(8,128)S(1)}, f32[3,32,512]{2,1,0:T(8,128)}, u32[]{:S(2)}) copy-start(f32[3,32,512]{2,1,0:T(8,128)} %param.2) | copy-start | bytes 589828
  1.1 3.8 %collective-permute-start = (f32[1,512]{1,0:T(1,128)S(1)}, f32[1,512]{1,0:T(1,128)S(1)}, u32[]{:S(2)}, u32[]{:S(2)}) collective-permute-start(f32[1,512]{1,0:T(1,128)S(1)} %get-tuple-element.68), channel_id=1, source_target_pairs={{1,0},{2,1},{3,2},{0,3},{5,4},{6,5},{7,6},{4,7},{9,8},{10,9},{11,1... | collective-permute-start | bytes 6152 | tf_op jit(solution)/shard_map/ppermute | solution.py:25
  3.6 3.0 %collective-permute-start.1 = (f32[1,512]{1,0:T(1,128)S(1)}, f32[1,512]{1,0:T(1,128)S(1)}, u32[]{:S(2)}, u32[]{:S(2)}) collective-permute-start(f32[1,512]{1,0:T(1,128)S(1)} %get-tuple-element.69), channel_id=1, source_target_pairs={{0,1},{1,2},{2,3},{3,0},{4,5},{5,6},{6,7},{7,4},{8,9},{9,10},{10,1... | collective-permute-start | bytes 6152 | tf_op jit(solution)/shard_map/ppermute | solution.py:23
  6.6 3.3 %copy-start = (f32[32,512]{1,0:T(8,128)S(1)}, f32[32,512]{1,0:T(8,128)}, u32[]{:S(2)}) copy-start(f32[32,512]{1,0:T(8,128)} %param.3) | copy-start | bytes 196612
  6.8 1.4 %collective-permute-start.2 = (f32[1,512]{1,0:T(1,128)S(1)}, f32[1,512]{1,0:T(1,128)S(1)}, u32[]{:S(2)}, u32[]{:S(2)}) collective-permute-start(f32[1,512]{1,0:T(1,128)S(1)} %get-tuple-element.66), channel_id=1, source_target_pairs={{1,0},{2,1},{3,2},{0,3},{5,4},{6,5},{7,6},{4,7},{9,8},{10,9},{11,1... | collective-permute-start | bytes 6152 | tf_op jit(solution)/shard_map/ppermute | solution.py:25
  6.8 3.1 %collective-permute-start.3 = (f32[1,512]{1,0:T(1,128)S(1)}, f32[1,512]{1,0:T(1,128)S(1)}, u32[]{:S(2)}, u32[]{:S(2)}) collective-permute-start(f32[1,512]{1,0:T(1,128)S(1)} %get-tuple-element.67), channel_id=1, source_target_pairs={{0,1},{1,2},{2,3},{3,0},{4,5},{5,6},{6,7},{7,4},{8,9},{9,10},{10,1... | collective-permute-start | bytes 6152 | tf_op jit(solution)/shard_map/ppermute | solution.py:23
  10.0 1.4 %collective-permute-start.4 = (f32[1,512]{1,0:T(1,128)S(1)}, f32[1,512]{1,0:T(1,128)S(1)}, u32[]{:S(2)}, u32[]{:S(2)}) collective-permute-start(f32[1,512]{1,0:T(1,128)S(1)} %get-tuple-element.64), channel_id=1, source_target_pairs={{1,0},{2,1},{3,2},{0,3},{5,4},{6,5},{7,6},{4,7},{9,8},{10,9},{11,1... | collective-permute-start | bytes 6152 | tf_op jit(solution)/shard_map/ppermute | solution.py:25
  10.0 3.1 %collective-permute-start.5 = (f32[1,512]{1,0:T(1,128)S(1)}, f32[1,512]{1,0:T(1,128)S(1)}, u32[]{:S(2)}, u32[]{:S(2)}) collective-permute-start(f32[1,512]{1,0:T(1,128)S(1)} %get-tuple-element.65), channel_id=1, source_target_pairs={{0,1},{1,2},{2,3},{3,0},{4,5},{5,6},{6,7},{7,4},{8,9},{9,10},{10,1... | collective-permute-start | bytes 6152 | tf_op jit(solution)/shard_map/ppermute | solution.py:23
  13.2 1.4 %collective-permute-start.6 = (f32[1,512]{1,0:T(1,128)S(1)}, f32[1,512]{1,0:T(1,128)S(1)}, u32[]{:S(2)}, u32[]{:S(2)}) collective-permute-start(f32[1,512]{1,0:T(1,128)S(1)} %get-tuple-element.62), channel_id=1, source_target_pairs={{1,0},{2,1},{3,2},{0,3},{5,4},{6,5},{7,6},{4,7},{9,8},{10,9},{11,1... | collective-permute-start | bytes 6152 | tf_op jit(solution)/shard_map/ppermute | solution.py:25
  13.3 3.1 %collective-permute-start.7 = (f32[1,512]{1,0:T(1,128)S(1)}, f32[1,512]{1,0:T(1,128)S(1)}, u32[]{:S(2)}, u32[]{:S(2)}) collective-permute-start(f32[1,512]{1,0:T(1,128)S(1)} %get-tuple-element.63), channel_id=1, source_target_pairs={{0,1},{1,2},{2,3},{3,0},{4,5},{5,6},{6,7},{7,4},{8,9},{9,10},{10,1... | collective-permute-start | bytes 6152 | tf_op jit(solution)/shard_map/ppermute | solution.py:23
  16.4 1.4 %collective-permute-start.8 = (f32[1,512]{1,0:T(1,128)S(1)}, f32[1,512]{1,0:T(1,128)S(1)}, u32[]{:S(2)}, u32[]{:S(2)}) collective-permute-start(f32[1,512]{1,0:T(1,128)S(1)} %get-tuple-element.60), channel_id=1, source_target_pairs={{1,0},{2,1},{3,2},{0,3},{5,4},{6,5},{7,6},{4,7},{9,8},{10,9},{11,1... | collective-permute-start | bytes 6152 | tf_op jit(solution)/shard_map/ppermute | solution.py:25
  16.5 3.1 %collective-permute-start.9 = (f32[1,512]{1,0:T(1,128)S(1)}, f32[1,512]{1,0:T(1,128)S(1)}, u32[]{:S(2)}, u32[]{:S(2)}) collective-permute-start(f32[1,512]{1,0:T(1,128)S(1)} %get-tuple-element.61), channel_id=1, source_target_pairs={{0,1},{1,2},{2,3},{3,0},{4,5},{5,6},{6,7},{7,4},{8,9},{9,10},{10,1... | collective-permute-start | bytes 6152 | tf_op jit(solution)/shard_map/ppermute | solution.py:23
  19.7 1.4 %collective-permute-start.10 = (f32[1,512]{1,0:T(1,128)S(1)}, f32[1,512]{1,0:T(1,128)S(1)}, u32[]{:S(2)}, u32[]{:S(2)}) collective-permute-start(f32[1,512]{1,0:T(1,128)S(1)} %get-tuple-element.58), channel_id=1, source_target_pairs={{1,0},{2,1},{3,2},{0,3},{5,4},{6,5},{7,6},{4,7},{9,8},{10,9},{11,1... | collective-permute-start | bytes 6152 | tf_op jit(solution)/shard_map/ppermute | solution.py:25
  19.7 3.1 %collective-permute-start.11 = (f32[1,512]{1,0:T(1,128)S(1)}, f32[1,512]{1,0:T(1,128)S(1)}, u32[]{:S(2)}, u32[]{:S(2)}) collective-permute-start(f32[1,512]{1,0:T(1,128)S(1)} %get-tuple-element.59), channel_id=1, source_target_pairs={{0,1},{1,2},{2,3},{3,0},{4,5},{5,6},{6,7},{7,4},{8,9},{9,10},{10,1... | collective-permute-start | bytes 6152 | tf_op jit(solution)/shard_map/ppermute | solution.py:23
  47.2 1.4 %collective-permute-start.12 = (f32[1,512]{1,0:T(1,128)S(1)}, f32[1,512]{1,0:T(1,128)S(1)}, u32[]{:S(2)}, u32[]{:S(2)}) collective-permute-start(f32[1,512]{1,0:T(1,128)S(1)} %get-tuple-element.56), channel_id=1, source_target_pairs={{1,0},{2,1},{3,2},{0,3},{5,4},{6,5},{7,6},{4,7},{9,8},{10,9},{11,1... | collective-permute-start | bytes 6152 | tf_op jit(solution)/shard_map/ppermute | solution.py:25
  47.2 3.1 %collective-permute-start.13 = (f32[1,512]{1,0:T(1,128)S(1)}, f32[1,512]{1,0:T(1,128)S(1)}, u32[]{:S(2)}, u32[]{:S(2)}) collective-permute-start(f32[1,512]{1,0:T(1,128)S(1)} %get-tuple-element.57), channel_id=1, source_target_pairs={{0,1},{1,2},{2,3},{3,0},{4,5},{5,6},{6,7},{7,4},{8,9},{9,10},{10,1... | collective-permute-start | bytes 6152 | tf_op jit(solution)/shard_map/ppermute | solution.py:23
  50.4 1.4 %collective-permute-start.14 = (f32[1,512]{1,0:T(1,128)S(1)}, f32[1,512]{1,0:T(1,128)S(1)}, u32[]{:S(2)}, u32[]{:S(2)}) collective-permute-start(f32[1,512]{1,0:T(1,128)S(1)} %get-tuple-element.54), channel_id=1, source_target_pairs={{1,0},{2,1},{3,2},{0,3},{5,4},{6,5},{7,6},{4,7},{9,8},{10,9},{11,1... | collective-permute-start | bytes 6152 | tf_op jit(solution)/shard_map/ppermute | solution.py:25
  50.5 3.1 %collective-permute-start.15 = (f32[1,512]{1,0:T(1,128)S(1)}, f32[1,512]{1,0:T(1,128)S(1)}, u32[]{:S(2)}, u32[]{:S(2)}) collective-permute-start(f32[1,512]{1,0:T(1,128)S(1)} %get-tuple-element.55), channel_id=1, source_target_pairs={{0,1},{1,2},{2,3},{3,0},{4,5},{5,6},{6,7},{7,4},{8,9},{9,10},{10,1... | collective-permute-start | bytes 6152 | tf_op jit(solution)/shard_map/ppermute | solution.py:23
  53.6 1.4 %collective-permute-start.16 = (f32[1,512]{1,0:T(1,128)S(1)}, f32[1,512]{1,0:T(1,128)S(1)}, u32[]{:S(2)}, u32[]{:S(2)}) collective-permute-start(f32[1,512]{1,0:T(1,128)S(1)} %get-tuple-element.52), channel_id=1, source_target_pairs={{1,0},{2,1},{3,2},{0,3},{5,4},{6,5},{7,6},{4,7},{9,8},{10,9},{11,1... | collective-permute-start | bytes 6152 | tf_op jit(solution)/shard_map/ppermute | solution.py:25
  53.7 3.1 %collective-permute-start.17 = (f32[1,512]{1,0:T(1,128)S(1)}, f32[1,512]{1,0:T(1,128)S(1)}, u32[]{:S(2)}, u32[]{:S(2)}) collective-permute-start(f32[1,512]{1,0:T(1,128)S(1)} %get-tuple-element.53), channel_id=1, source_target_pairs={{0,1},{1,2},{2,3},{3,0},{4,5},{5,6},{6,7},{7,4},{8,9},{9,10},{10,1... | collective-permute-start | bytes 6152 | tf_op jit(solution)/shard_map/ppermute | solution.py:23
  56.9 1.4 %collective-permute-start.18 = (f32[1,512]{1,0:T(1,128)S(1)}, f32[1,512]{1,0:T(1,128)S(1)}, u32[]{:S(2)}, u32[]{:S(2)}) collective-permute-start(f32[1,512]{1,0:T(1,128)S(1)} %get-tuple-element.50), channel_id=1, source_target_pairs={{1,0},{2,1},{3,2},{0,3},{5,4},{6,5},{7,6},{4,7},{9,8},{10,9},{11,1... | collective-permute-start | bytes 6152 | tf_op jit(solution)/shard_map/ppermute | solution.py:25
  56.9 3.1 %collective-permute-start.19 = (f32[1,512]{1,0:T(1,128)S(1)}, f32[1,512]{1,0:T(1,128)S(1)}, u32[]{:S(2)}, u32[]{:S(2)}) collective-permute-start(f32[1,512]{1,0:T(1,128)S(1)} %get-tuple-element.51), channel_id=1, source_target_pairs={{0,1},{1,2},{2,3},{3,0},{4,5},{5,6},{6,7},{7,4},{8,9},{9,10},{10,1... | collective-permute-start | bytes 6152 | tf_op jit(solution)/shard_map/ppermute | solution.py:23
  60.0 1.4 %collective-permute-start.20 = (f32[1,512]{1,0:T(1,128)S(1)}, f32[1,512]{1,0:T(1,128)S(1)}, u32[]{:S(2)}, u32[]{:S(2)}) collective-permute-start(f32[1,512]{1,0:T(1,128)S(1)} %get-tuple-element.48), channel_id=1, source_target_pairs={{1,0},{2,1},{3,2},{0,3},{5,4},{6,5},{7,6},{4,7},{9,8},{10,9},{11,1... | collective-permute-start | bytes 6152 | tf_op jit(solution)/shard_map/ppermute | solution.py:25
  60.1 3.1 %collective-permute-start.21 = (f32[1,512]{1,0:T(1,128)S(1)}, f32[1,512]{1,0:T(1,128)S(1)}, u32[]{:S(2)}, u32[]{:S(2)}) collective-permute-start(f32[1,512]{1,0:T(1,128)S(1)} %get-tuple-element.49), channel_id=1, source_target_pairs={{0,1},{1,2},{2,3},{3,0},{4,5},{5,6},{6,7},{7,4},{8,9},{9,10},{10,1... | collective-permute-start | bytes 6152 | tf_op jit(solution)/shard_map/ppermute | solution.py:23
  63.3 1.4 %collective-permute-start.22 = (f32[1,512]{1,0:T(1,128)S(1)}, f32[1,512]{1,0:T(1,128)S(1)}, u32[]{:S(2)}, u32[]{:S(2)}) collective-permute-start(f32[1,512]{1,0:T(1,128)S(1)} %get-tuple-element.46), channel_id=1, source_target_pairs={{1,0},{2,1},{3,2},{0,3},{5,4},{6,5},{7,6},{4,7},{9,8},{10,9},{11,1... | collective-permute-start | bytes 6152 | tf_op jit(solution)/shard_map/ppermute | solution.py:25
  63.4 3.1 %collective-permute-start.23 = (f32[1,512]{1,0:T(1,128)S(1)}, f32[1,512]{1,0:T(1,128)S(1)}, u32[]{:S(2)}, u32[]{:S(2)}) collective-permute-start(f32[1,512]{1,0:T(1,128)S(1)} %get-tuple-element.47), channel_id=1, source_target_pairs={{0,1},{1,2},{2,3},{3,0},{4,5},{5,6},{6,7},{7,4},{8,9},{9,10},{10,1... | collective-permute-start | bytes 6152 | tf_op jit(solution)/shard_map/ppermute | solution.py:23
  78.6 11.1 %all-to-all-start.3 = ((f32[8,3,4,512]{3,2,1,0:T(4,128)}), f32[8,3,4,512]{3,2,1,0:T(4,128)S(1)}, u32[]{:S(2)}, u32[]{:S(2)}) async-start(f32[8,3,4,512]{3,2,1,0:T(4,128)} %concatenate.115.clone), calls=%async_computation.3 | async-start | bytes 393216 | tf_op jit(solution)/shard_map/all_to_all | solution.py:106
where the time goes:
time: 90.9 us; the launch traced here: 90.6 us
  waiting for transfers between devices  38 us (42%)
  blocking collectives  34.5 us (38%)
  starting transfers between devices  12 us (13%)
  other arithmetic  4.07 us (4%)
  local copies, waits for them, and re-layouts  1.53 us (2%)
    all_to_all x2, blocking collectives, body(): lax.all_to_all(carried[None], 'tm', split_axis=2, concat_axis=0, tiled=True)  24.3 us
    ppermute x12, waiting for transfers between devices, padded_2(): lax.ppermute(tail, axis, [(i, (i + 1) % count) for i in range(count)])  21.1 us
    all_to_all x1, blocking collectives, body(): lax.all_to_all(running, 'tm', split_axis=0, concat_axis=2, tiled=True)[0]  10.2 us
    ppermute x12, waiting for transfers between devices, padded_2(): lax.ppermute(head, axis, [((i + 1) % count, i) for i in range(count)])  9.29 us
    all_to_all x1, waiting for transfers between devices, body(): lax.all_to_all(running, 'tm', split_axis=0, concat_axis=2, tiled=True)[0]  7.62 us
    ppermute x12, starting transfers between devices, padded_2(): lax.ppermute(tail, axis, [(i, (i + 1) % count) for i in range(count)])  5.47 us
    all_to_all x1, starting transfers between devices, body(): lax.all_to_all(running, 'tm', split_axis=0, concat_axis=2, tiled=True)[0]  3.39 us
    ppermute x12, starting transfers between devices, padded_2(): lax.ppermute(head, axis, [((i + 1) % count, i) for i in range(count)])  3.12 us
  transfers between devices with their start and end apart: 25, of which 25 were waited for; matrix products, arithmetic and copies ran while one was open for 1% of the time, Pallas kernels for 0%

commit v1 on v0

--- a/solution.py
+++ b/solution.py
@@ -103,7 +103,10 @@
         stacked = lax.all_to_all(carried[None], "tm", split_axis=2, concat_axis=0, tiled=True)
         running = jnp.cumsum(stacked, axis=0)
         running = jnp.concatenate([jnp.zeros_like(stacked[:1]), running[:-1]], axis=0)
-        before = lax.all_to_all(running, "tm", split_axis=0, concat_axis=2, tiled=True)[0]
+        before = jnp.concatenate(
+            lax.all_to_all(jnp.stack(jnp.split(running, lax.axis_size("tm"), axis=0)), "tm", 0, 0),
+            axis=2,
+        )[0]
         total = start + before
         if round_index + 1 < ROUNDS:
             guess = rotate(total, number * turning)

time: 90.9 us -> 96.4 us (1.061)
  blocking collectives: 34.5 us -> 10.2 us
  waiting for transfers between devices: 38 us -> 53 us
  starting transfers between devices: 12 us -> 21.2 us
  local copies, waits for them, and re-layouts: 1.53 us -> 7.04 us
    all_to_all x3 -> x1, blocking collectives: 34.5 us -> 10.2 us  [body(): lax.all_to_all(jnp.stack(jnp.split(running, lax.axis_size('tm'), axis=0))...]
    all_to_all x1 -> x3, waiting for transfers between devices: 7.62 us -> 22.6 us  [the longest x2 15 us: body(): lax.all_to_all(carried[None], 'tm', split_axis=2, concat_axis=0, tiled=True)]
    all_to_all x1 -> x3, starting transfers between devices: 3.39 us -> 12.6 us  [the longest x2 9.2 us: body(): lax.all_to_all(carried[None], 'tm', split_axis=2, concat_axis=0, tiled=True)]
    unnamed x6 -> x18, local copies, waits for them, and re-layouts: 0.04 us -> 4.35 us
    broadcast_in_dim x2, local copies, waits for them, and re-layouts: 0.41 us -> 1.76 us  [body(): carried[None]]
  transfers between devices with their start and end apart: 25 -> 27, of which waited for: 25 -> 27; matrix products, arithmetic and copies ran while one was open for 1% -> 2% of each run, Pallas kernels for 0% -> 0%
where the time goes in v1:
time: 96.4 us; the launch traced here: 96 us
  waiting for transfers between devices  53 us (55%)
  starting transfers between devices  21.2 us (22%)
  blocking collectives  10.2 us (11%)
  local copies, waits for them, and re-layouts  7.04 us (7%)
  other arithmetic  4.07 us (4%)
    ppermute x12, waiting for transfers between devices, padded_2(): lax.ppermute(tail, axis, [(i, (i + 1) % count) for i in range(count)])  21.1 us
    all_to_all x2, waiting for transfers between devices, body(): lax.all_to_all(carried[None], 'tm', split_axis=2, concat_axis=0, tiled=True)  15 us
    all_to_all x1, blocking collectives, body(): lax.all_to_all(jnp.stack(jnp.split(running, lax.axis_size('tm'), axis=0))...  10.2 us
    ppermute x12, waiting for transfers between devices, padded_2(): lax.ppermute(head, axis, [((i + 1) % count, i) for i in range(count)])  9.29 us
    all_to_all x2, starting transfers between devices, body(): lax.all_to_all(carried[None], 'tm', split_axis=2, concat_axis=0, tiled=True)  9.2 us
    all_to_all x1, waiting for transfers between devices, body(): lax.all_to_all(jnp.stack(jnp.split(running, lax.axis_size('tm'), axis=0))...  7.63 us
    ppermute x12, starting transfers between devices, padded_2(): lax.ppermute(tail, axis, [(i, (i + 1) % count) for i in range(count)])  5.47 us
    unnamed x18, local copies, waits for them, and re-layouts  4.35 us
  transfers between devices with their start and end apart: 27, of which 27 were waited for; matrix products, arithmetic and copies ran while one was open for 2% of the time, Pallas kernels for 0%

profile of v1, /device:TPU:0, one launch (start us, length us, event | category | flops | bytes accessed | tf_op | source)
XLA Modules:
  0.0 96.0 jit_solution(14518451957335326506)
XLA Ops:
  0.2 1.0 %multiply_multiply_fusion.5 = (f32[32,512]{1,0:T(8,128)S(1)}, f32[32,512]{1,0:T(8,128)S(1)}, f32[32,512]{1,0:T(8,128)S(1)}) fusion(f32[32,512]{1,0:T(8,128)} %param.3, f32[512]{0:T(512)S(1)} %fusion.117, f32[512]{0:T(512)S(1)} %get-tuple-element.70, f32[3,32,512]{2,1,0:T(8,128)} %param.2, f32[512]{0:T(512)S(1)} %get-tuple-element.71), kind=kLoop, calls=%fused_computation.196 | loop fusion | flops 147456 | bytes 399360 | tf_op jit(solution)/shard_map/mul | solution.py:59
  1.1 2.5 %collective-permute-start = (f32[1,512]{1,0:T(1,128)S(1)}, f32[1,512]{1,0:T(1,128)S(1)}, u32[]{:S(2)}, u32[]{:S(2)}) collective-permute-start(f32[1,512]{1,0:T(1,128)S(1)} %get-tuple-element.68), channel_id=1, source_target_pairs={{1,0},{2,1},{3,2},{0,3},{5,4},{6,5},{7,6},{4,7},{9,8},{10,9},{11,1... | collective-permute-start | bytes 6152 | tf_op jit(solution)/shard_map/ppermute | solution.py:25
  3.8 1.1 %collective-permute-done = f32[1,512]{1,0:T(1,128)S(1)} collective-permute-done((f32[1,512]{1,0:T(1,128)S(1)}, f32[1,512]{1,0:T(1,128)S(1)}, u32[]{:S(2)}, u32[]{:S(2)}) %collective-permute-start) | collective-permute-done | bytes 2080 | tf_op jit(solution)/shard_map/ppermute | solution.py:25
  4.9 1.7 %collective-permute-done.1 = f32[1,512]{1,0:T(1,128)S(1)} collective-permute-done((f32[1,512]{1,0:T(1,128)S(1)}, f32[1,512]{1,0:T(1,128)S(1)}, u32[]{:S(2)}, u32[]{:S(2)}) %collective-permute-start.1) | collective-permute-done | bytes 2080 | tf_op jit(solution)/shard_map/ppermute | solution.py:23
  7.4 0.8 collective-permute-done.2
  8.1 1.8 %collective-permute-done.3 = f32[1,512]{1,0:T(1,128)S(1)} collective-permute-done((f32[1,512]{1,0:T(1,128)S(1)}, f32[1,512]{1,0:T(1,128)S(1)}, u32[]{:S(2)}, u32[]{:S(2)}) %collective-permute-start.3) | collective-permute-done | bytes 2080 | tf_op jit(solution)/shard_map/ppermute | solution.py:23
  11.3 1.8 %collective-permute-done.5 = f32[1,512]{1,0:T(1,128)S(1)} collective-permute-done((f32[1,512]{1,0:T(1,128)S(1)}, f32[1,512]{1,0:T(1,128)S(1)}, u32[]{:S(2)}, u32[]{:S(2)}) %collective-permute-start.5) | collective-permute-done | bytes 2080 | tf_op jit(solution)/shard_map/ppermute | solution.py:23
  13.8 0.8 collective-permute-done.6
  14.6 1.8 %collective-permute-done.7 = f32[1,512]{1,0:T(1,128)S(1)} collective-permute-done((f32[1,512]{1,0:T(1,128)S(1)}, f32[1,512]{1,0:T(1,128)S(1)}, u32[]{:S(2)}, u32[]{:S(2)}) %collective-permute-start.7) | collective-permute-done | bytes 2080 | tf_op jit(solution)/shard_map/ppermute | solution.py:23
  17.8 1.8 %collective-permute-done.9 = f32[1,512]{1,0:T(1,128)S(1)} collective-permute-done((f32[1,512]{1,0:T(1,128)S(1)}, f32[1,512]{1,0:T(1,128)S(1)}, u32[]{:S(2)}, u32[]{:S(2)}) %collective-permute-start.9) | collective-permute-done | bytes 2080 | tf_op jit(solution)/shard_map/ppermute | solution.py:23
  20.3 0.7 collective-permute-done.10
  21.0 1.8 %collective-permute-done.11 = f32[1,512]{1,0:T(1,128)S(1)} collective-permute-done((f32[1,512]{1,0:T(1,128)S(1)}, f32[1,512]{1,0:T(1,128)S(1)}, u32[]{:S(2)}, u32[]{:S(2)}) %collective-permute-start.11) | collective-permute-done | bytes 2080 | tf_op jit(solution)/shard_map/ppermute | solution.py:23
  23.0 0.9 copy.80
  23.9 5.8 %all-to-all-start = ((f32[1,3,32,512]{3,0,1,2:T(1,128)}), f32[1,3,32,512]{3,0,1,2:T(1,128)S(1)}, u32[]{:S(2)}, u32[]{:S(2)}) async-start(f32[1,3,32,512]{3,0,1,2:T(1,128)} %copy.80), calls=%async_computation | async-start | bytes 393216 | tf_op jit(solution)/shard_map/all_to_all | solution.py:103
  29.7 7.8 %all-to-all-done = f32[1,3,32,512]{3,0,1,2:T(1,128)S(1)} async-done(((f32[1,3,32,512]{3,0,1,2:T(1,128)}), f32[1,3,32,512]{3,0,1,2:T(1,128)S(1)}, u32[]{:S(2)}, u32[]{:S(2)}) %all-to-all-start) | async-done | bytes 196640 | tf_op jit(solution)/shard_map/all_to_all | solution.py:103
  37.7 10.2 %all_to_all.46 = f32[8,1,3,4,512]{4,3,2,1,0:T(4,128)S(1)} all-to-all(f32[8,1,3,4,512]{4,3,2,1,0:T(4,128)S(1)} %constant_dynamic-update-slice_fusion), channel_id=1, replica_groups=mesh['tm'=8,'lon'=4] {'tm'}, dimensions={0} | all-to-all | bytes 393216 | tf_op jit(solution)/shard_map/all_to_all | solution.py:107
  48.6 0.8 collective-permute-done.12
  49.4 1.8 %collective-permute-done.13 = f32[1,512]{1,0:T(1,128)S(1)} collective-permute-done((f32[1,512]{1,0:T(1,128)S(1)}, f32[1,512]{1,0:T(1,128)S(1)}, u32[]{:S(2)}, u32[]{:S(2)}) %collective-permute-start.13) | collective-permute-done | bytes 2080 | tf_op jit(solution)/shard_map/ppermute | solution.py:23
  51.9 0.8 collective-permute-done.14
  52.7 1.8 %collective-permute-done.15 = f32[1,512]{1,0:T(1,128)S(1)} collective-permute-done((f32[1,512]{1,0:T(1,128)S(1)}, f32[1,512]{1,0:T(1,128)S(1)}, u32[]{:S(2)}, u32[]{:S(2)}) %collective-permute-start.15) | collective-permute-done | bytes 2080 | tf_op jit(solution)/shard_map/ppermute | solution.py:23
  55.9 1.8 %collective-permute-done.17 = f32[1,512]{1,0:T(1,128)S(1)} collective-permute-done((f32[1,512]{1,0:T(1,128)S(1)}, f32[1,512]{1,0:T(1,128)S(1)}, u32[]{:S(2)}, u32[]{:S(2)}) %collective-permute-start.17) | collective-permute-done | bytes 2080 | tf_op jit(solution)/shard_map/ppermute | solution.py:23
  58.3 0.8 collective-permute-done.18
  59.1 1.8 %collective-permute-done.19 = f32[1,512]{1,0:T(1,128)S(1)} collective-permute-done((f32[1,512]{1,0:T(1,128)S(1)}, f32[1,512]{1,0:T(1,128)S(1)}, u32[]{:S(2)}, u32[]{:S(2)}) %collective-permute-start.19) | collective-permute-done | bytes 2080 | tf_op jit(solution)/shard_map/ppermute | solution.py:23
  61.6 0.7 collective-permute-done.20
  62.3 1.8 %collective-permute-done.21 = f32[1,512]{1,0:T(1,128)S(1)} collective-permute-done((f32[1,512]{1,0:T(1,128)S(1)}, f32[1,512]{1,0:T(1,128)S(1)}, u32[]{:S(2)}, u32[]{:S(2)}) %collective-permute-start.21) | collective-permute-done | bytes 2080 | tf_op jit(solution)/shard_map/ppermute | solution.py:23
  64.8 0.8 collective-permute-done.22
  65.5 1.8 %collective-permute-done.23 = f32[1,512]{1,0:T(1,128)S(1)} collective-permute-done((f32[1,512]{1,0:T(1,128)S(1)}, f32[1,512]{1,0:T(1,128)S(1)}, u32[]{:S(2)}, u32[]{:S(2)}) %collective-permute-start.23) | collective-permute-done | bytes 2080 | tf_op jit(solution)/shard_map/ppermute | solution.py:23
  67.5 0.9 copy.89
  68.4 3.4 %all-to-all-start.2 = ((f32[1,3,32,512]{3,0,1,2:T(1,128)}), f32[1,3,32,512]{3,0,1,2:T(1,128)S(1)}, u32[]{:S(2)}, u32[]{:S(2)}) async-start(f32[1,3,32,512]{3,0,1,2:T(1,128)} %copy.89), calls=%async_computation.2 | async-start | bytes 393216 | tf_op jit(solution)/shard_map/all_to_all | solution.py:103
  72.4 7.2 %all-to-all-done.2 = f32[1,3,32,512]{3,0,1,2:T(1,128)S(1)} async-done(((f32[1,3,32,512]{3,0,1,2:T(1,128)}), f32[1,3,32,512]{3,0,1,2:T(1,128)S(1)}, u32[]{:S(2)}, u32[]{:S(2)}) %all-to-all-start.2) | async-done | bytes 196640 | tf_op jit(solution)/shard_map/all_to_all | solution.py:103
  84.0 3.4 %all-to-all-start.3 = ((f32[8,1,3,4,512]{4,3,2,1,0:T(4,128)}), f32[8,1,3,4,512]{4,3,2,1,0:T(4,128)S(1)}, u32[]{:S(2)}, u32[]{:S(2)}) async-start(f32[8,1,3,4,512]{4,3,2,1,0:T(4,128)} %constant_dynamic-update-slice_fusion.8), calls=%async_computation.3 | async-start | bytes 393216 | tf_op jit(solution)/shard_map/all_to_all | solution.py:107
  87.5 7.6 %all-to-all-done.3 = f32[8,1,3,4,512]{4,3,2,1,0:T(4,128)S(1)} async-done(((f32[8,1,3,4,512]{4,3,2,1,0:T(4,128)}), f32[8,1,3,4,512]{4,3,2,1,0:T(4,128)S(1)}, u32[]{:S(2)}, u32[]{:S(2)}) %all-to-all-start.3) | async-done | bytes 196640 | tf_op jit(solution)/shard_map/all_to_all | solution.py:107
  (103 shorter events, 16.6 us)
Async XLA Ops:
  0.1 6.5 %copy-start.1 = (f32[3,32,512]{2,1,0:T(8,128)S(1)}, f32[3,32,512]{2,1,0:T(8,128)}, u32[]{:S(2)}) copy-start(f32[3,32,512]{2,1,0:T(8,128)} %param.2) | copy-start | bytes 589828
  1.1 3.8 %collective-permute-start = (f32[1,512]{1,0:T(1,128)S(1)}, f32[1,512]{1,0:T(1,128)S(1)}, u32[]{:S(2)}, u32[]{:S(2)}) collective-permute-start(f32[1,512]{1,0:T(1,128)S(1)} %get-tuple-element.68), channel_id=1, source_target_pairs={{1,0},{2,1},{3,2},{0,3},{5,4},{6,5},{7,6},{4,7},{9,8},{10,9},{11,1... | collective-permute-start | bytes 6152 | tf_op jit(solution)/shard_map/ppermute | solution.py:25
  3.6 3.0 %collective-permute-start.1 = (f32[1,512]{1,0:T(1,128)S(1)}, f32[1,512]{1,0:T(1,128)S(1)}, u32[]{:S(2)}, u32[]{:S(2)}) collective-permute-start(f32[1,512]{1,0:T(1,128)S(1)} %get-tuple-element.69), channel_id=1, source_target_pairs={{0,1},{1,2},{2,3},{3,0},{4,5},{5,6},{6,7},{7,4},{8,9},{9,10},{10,1... | collective-permute-start | bytes 6152 | tf_op jit(solution)/shard_map/ppermute | solution.py:23
  6.6 3.3 %copy-start = (f32[32,512]{1,0:T(8,128)S(1)}, f32[32,512]{1,0:T(8,128)}, u32[]{:S(2)}) copy-start(f32[32,512]{1,0:T(8,128)} %param.3) | copy-start | bytes 196612
  6.8 1.4 %collective-permute-start.2 = (f32[1,512]{1,0:T(1,128)S(1)}, f32[1,512]{1,0:T(1,128)S(1)}, u32[]{:S(2)}, u32[]{:S(2)}) collective-permute-start(f32[1,512]{1,0:T(1,128)S(1)} %get-tuple-element.66), channel_id=1, source_target_pairs={{1,0},{2,1},{3,2},{0,3},{5,4},{6,5},{7,6},{4,7},{9,8},{10,9},{11,1... | collective-permute-start | bytes 6152 | tf_op jit(solution)/shard_map/ppermute | solution.py:25
  6.8 3.1 %collective-permute-start.3 = (f32[1,512]{1,0:T(1,128)S(1)}, f32[1,512]{1,0:T(1,128)S(1)}, u32[]{:S(2)}, u32[]{:S(2)}) collective-permute-start(f32[1,512]{1,0:T(1,128)S(1)} %get-tuple-element.67), channel_id=1, source_target_pairs={{0,1},{1,2},{2,3},{3,0},{4,5},{5,6},{6,7},{7,4},{8,9},{9,10},{10,1... | collective-permute-start | bytes 6152 | tf_op jit(solution)/shard_map/ppermute | solution.py:23
  10.0 1.4 %collective-permute-start.4 = (f32[1,512]{1,0:T(1,128)S(1)}, f32[1,512]{1,0:T(1,128)S(1)}, u32[]{:S(2)}, u32[]{:S(2)}) collective-permute-start(f32[1,512]{1,0:T(1,128)S(1)} %get-tuple-element.64), channel_id=1, source_target_pairs={{1,0},{2,1},{3,2},{0,3},{5,4},{6,5},{7,6},{4,7},{9,8},{10,9},{11,1... | collective-permute-start | bytes 6152 | tf_op jit(solution)/shard_map/ppermute | solution.py:25
  10.0 3.1 %collective-permute-start.5 = (f32[1,512]{1,0:T(1,128)S(1)}, f32[1,512]{1,0:T(1,128)S(1)}, u32[]{:S(2)}, u32[]{:S(2)}) collective-permute-start(f32[1,512]{1,0:T(1,128)S(1)} %get-tuple-element.65), channel_id=1, source_target_pairs={{0,1},{1,2},{2,3},{3,0},{4,5},{5,6},{6,7},{7,4},{8,9},{9,10},{10,1... | collective-permute-start | bytes 6152 | tf_op jit(solution)/shard_map/ppermute | solution.py:23
  13.2 1.4 %collective-permute-start.6 = (f32[1,512]{1,0:T(1,128)S(1)}, f32[1,512]{1,0:T(1,128)S(1)}, u32[]{:S(2)}, u32[]{:S(2)}) collective-permute-start(f32[1,512]{1,0:T(1,128)S(1)} %get-tuple-element.62), channel_id=1, source_target_pairs={{1,0},{2,1},{3,2},{0,3},{5,4},{6,5},{7,6},{4,7},{9,8},{10,9},{11,1... | collective-permute-start | bytes 6152 | tf_op jit(solution)/shard_map/ppermute | solution.py:25
  13.3 3.1 %collective-permute-start.7 = (f32[1,512]{1,0:T(1,128)S(1)}, f32[1,512]{1,0:T(1,128)S(1)}, u32[]{:S(2)}, u32[]{:S(2)}) collective-permute-start(f32[1,512]{1,0:T(1,128)S(1)} %get-tuple-element.63), channel_id=1, source_target_pairs={{0,1},{1,2},{2,3},{3,0},{4,5},{5,6},{6,7},{7,4},{8,9},{9,10},{10,1... | collective-permute-start | bytes 6152 | tf_op jit(solution)/shard_map/ppermute | solution.py:23
  16.4 1.4 %collective-permute-start.8 = (f32[1,512]{1,0:T(1,128)S(1)}, f32[1,512]{1,0:T(1,128)S(1)}, u32[]{:S(2)}, u32[]{:S(2)}) collective-permute-start(f32[1,512]{1,0:T(1,128)S(1)} %get-tuple-element.60), channel_id=1, source_target_pairs={{1,0},{2,1},{3,2},{0,3},{5,4},{6,5},{7,6},{4,7},{9,8},{10,9},{11,1... | collective-permute-start | bytes 6152 | tf_op jit(solution)/shard_map/ppermute | solution.py:25
  16.5 3.1 %collective-permute-start.9 = (f32[1,512]{1,0:T(1,128)S(1)}, f32[1,512]{1,0:T(1,128)S(1)}, u32[]{:S(2)}, u32[]{:S(2)}) collective-permute-start(f32[1,512]{1,0:T(1,128)S(1)} %get-tuple-element.61), channel_id=1, source_target_pairs={{0,1},{1,2},{2,3},{3,0},{4,5},{5,6},{6,7},{7,4},{8,9},{9,10},{10,1... | collective-permute-start | bytes 6152 | tf_op jit(solution)/shard_map/ppermute | solution.py:23
  19.7 1.4 %collective-permute-start.10 = (f32[1,512]{1,0:T(1,128)S(1)}, f32[1,512]{1,0:T(1,128)S(1)}, u32[]{:S(2)}, u32[]{:S(2)}) collective-permute-start(f32[1,512]{1,0:T(1,128)S(1)} %get-tuple-element.58), channel_id=1, source_target_pairs={{1,0},{2,1},{3,2},{0,3},{5,4},{6,5},{7,6},{4,7},{9,8},{10,9},{11,1... | collective-permute-start | bytes 6152 | tf_op jit(solution)/shard_map/ppermute | solution.py:25
  19.7 3.1 %collective-permute-start.11 = (f32[1,512]{1,0:T(1,128)S(1)}, f32[1,512]{1,0:T(1,128)S(1)}, u32[]{:S(2)}, u32[]{:S(2)}) collective-permute-start(f32[1,512]{1,0:T(1,128)S(1)} %get-tuple-element.59), channel_id=1, source_target_pairs={{0,1},{1,2},{2,3},{3,0},{4,5},{5,6},{6,7},{7,4},{8,9},{9,10},{10,1... | collective-permute-start | bytes 6152 | tf_op jit(solution)/shard_map/ppermute | solution.py:23
  23.9 13.6 %all-to-all-start = ((f32[1,3,32,512]{3,0,1,2:T(1,128)}), f32[1,3,32,512]{3,0,1,2:T(1,128)S(1)}, u32[]{:S(2)}, u32[]{:S(2)}) async-start(f32[1,3,32,512]{3,0,1,2:T(1,128)} %copy.80), calls=%async_computation | async-start | bytes 393216 | tf_op jit(solution)/shard_map/all_to_all | solution.py:103
  48.0 1.4 %collective-permute-start.12 = (f32[1,512]{1,0:T(1,128)S(1)}, f32[1,512]{1,0:T(1,128)S(1)}, u32[]{:S(2)}, u32[]{:S(2)}) collective-permute-start(f32[1,512]{1,0:T(1,128)S(1)} %get-tuple-element.56), channel_id=1, source_target_pairs={{1,0},{2,1},{3,2},{0,3},{5,4},{6,5},{7,6},{4,7},{9,8},{10,9},{11,1... | collective-permute-start | bytes 6152 | tf_op jit(solution)/shard_map/ppermute | solution.py:25
  48.1 3.1 %collective-permute-start.13 = (f32[1,512]{1,0:T(1,128)S(1)}, f32[1,512]{1,0:T(1,128)S(1)}, u32[]{:S(2)}, u32[]{:S(2)}) collective-permute-start(f32[1,512]{1,0:T(1,128)S(1)} %get-tuple-element.57), channel_id=1, source_target_pairs={{0,1},{1,2},{2,3},{3,0},{4,5},{5,6},{6,7},{7,4},{8,9},{9,10},{10,1... | collective-permute-start | bytes 6152 | tf_op jit(solution)/shard_map/ppermute | solution.py:23
  51.3 1.4 %collective-permute-start.14 = (f32[1,512]{1,0:T(1,128)S(1)}, f32[1,512]{1,0:T(1,128)S(1)}, u32[]{:S(2)}, u32[]{:S(2)}) collective-permute-start(f32[1,512]{1,0:T(1,128)S(1)} %get-tuple-element.54), channel_id=1, source_target_pairs={{1,0},{2,1},{3,2},{0,3},{5,4},{6,5},{7,6},{4,7},{9,8},{10,9},{11,1... | collective-permute-start | bytes 6152 | tf_op jit(solution)/shard_map/ppermute | solution.py:25
  51.4 3.1 %collective-permute-start.15 = (f32[1,512]{1,0:T(1,128)S(1)}, f32[1,512]{1,0:T(1,128)S(1)}, u32[]{:S(2)}, u32[]{:S(2)}) collective-permute-start(f32[1,512]{1,0:T(1,128)S(1)} %get-tuple-element.55), channel_id=1, source_target_pairs={{0,1},{1,2},{2,3},{3,0},{4,5},{5,6},{6,7},{7,4},{8,9},{9,10},{10,1... | collective-permute-start | bytes 6152 | tf_op jit(solution)/shard_map/ppermute | solution.py:23
  54.5 1.4 %collective-permute-start.16 = (f32[1,512]{1,0:T(1,128)S(1)}, f32[1,512]{1,0:T(1,128)S(1)}, u32[]{:S(2)}, u32[]{:S(2)}) collective-permute-start(f32[1,512]{1,0:T(1,128)S(1)} %get-tuple-element.52), channel_id=1, source_target_pairs={{1,0},{2,1},{3,2},{0,3},{5,4},{6,5},{7,6},{4,7},{9,8},{10,9},{11,1... | collective-permute-start | bytes 6152 | tf_op jit(solution)/shard_map/ppermute | solution.py:25
  54.6 3.1 %collective-permute-start.17 = (f32[1,512]{1,0:T(1,128)S(1)}, f32[1,512]{1,0:T(1,128)S(1)}, u32[]{:S(2)}, u32[]{:S(2)}) collective-permute-start(f32[1,512]{1,0:T(1,128)S(1)} %get-tuple-element.53), channel_id=1, source_target_pairs={{0,1},{1,2},{2,3},{3,0},{4,5},{5,6},{6,7},{7,4},{8,9},{9,10},{10,1... | collective-permute-start | bytes 6152 | tf_op jit(solution)/shard_map/ppermute | solution.py:23
  57.7 1.4 %collective-permute-start.18 = (f32[1,512]{1,0:T(1,128)S(1)}, f32[1,512]{1,0:T(1,128)S(1)}, u32[]{:S(2)}, u32[]{:S(2)}) collective-permute-start(f32[1,512]{1,0:T(1,128)S(1)} %get-tuple-element.50), channel_id=1, source_target_pairs={{1,0},{2,1},{3,2},{0,3},{5,4},{6,5},{7,6},{4,7},{9,8},{10,9},{11,1... | collective-permute-start | bytes 6152 | tf_op jit(solution)/shard_map/ppermute | solution.py:25
  57.8 3.1 %collective-permute-start.19 = (f32[1,512]{1,0:T(1,128)S(1)}, f32[1,512]{1,0:T(1,128)S(1)}, u32[]{:S(2)}, u32[]{:S(2)}) collective-permute-start(f32[1,512]{1,0:T(1,128)S(1)} %get-tuple-element.51), channel_id=1, source_target_pairs={{0,1},{1,2},{2,3},{3,0},{4,5},{5,6},{6,7},{7,4},{8,9},{9,10},{10,1... | collective-permute-start | bytes 6152 | tf_op jit(solution)/shard_map/ppermute | solution.py:23
  60.9 1.4 %collective-permute-start.20 = (f32[1,512]{1,0:T(1,128)S(1)}, f32[1,512]{1,0:T(1,128)S(1)}, u32[]{:S(2)}, u32[]{:S(2)}) collective-permute-start(f32[1,512]{1,0:T(1,128)S(1)} %get-tuple-element.48), channel_id=1, source_target_pairs={{1,0},{2,1},{3,2},{0,3},{5,4},{6,5},{7,6},{4,7},{9,8},{10,9},{11,1... | collective-permute-start | bytes 6152 | tf_op jit(solution)/shard_map/ppermute | solution.py:25
  61.0 3.1 %collective-permute-start.21 = (f32[1,512]{1,0:T(1,128)S(1)}, f32[1,512]{1,0:T(1,128)S(1)}, u32[]{:S(2)}, u32[]{:S(2)}) collective-permute-start(f32[1,512]{1,0:T(1,128)S(1)} %get-tuple-element.49), channel_id=1, source_target_pairs={{0,1},{1,2},{2,3},{3,0},{4,5},{5,6},{6,7},{7,4},{8,9},{9,10},{10,1... | collective-permute-start | bytes 6152 | tf_op jit(solution)/shard_map/ppermute | solution.py:23
  64.2 1.4 %collective-permute-start.22 = (f32[1,512]{1,0:T(1,128)S(1)}, f32[1,512]{1,0:T(1,128)S(1)}, u32[]{:S(2)}, u32[]{:S(2)}) collective-permute-start(f32[1,512]{1,0:T(1,128)S(1)} %get-tuple-element.46), channel_id=1, source_target_pairs={{1,0},{2,1},{3,2},{0,3},{5,4},{6,5},{7,6},{4,7},{9,8},{10,9},{11,1... | collective-permute-start | bytes 6152 | tf_op jit(solution)/shard_map/ppermute | solution.py:25
  64.2 3.1 %collective-permute-start.23 = (f32[1,512]{1,0:T(1,128)S(1)}, f32[1,512]{1,0:T(1,128)S(1)}, u32[]{:S(2)}, u32[]{:S(2)}) collective-permute-start(f32[1,512]{1,0:T(1,128)S(1)} %get-tuple-element.47), channel_id=1, source_target_pairs={{0,1},{1,2},{2,3},{3,0},{4,5},{5,6},{6,7},{7,4},{8,9},{9,10},{10,1... | collective-permute-start | bytes 6152 | tf_op jit(solution)/shard_map/ppermute | solution.py:23
  68.4 11.2 %all-to-all-start.2 = ((f32[1,3,32,512]{3,0,1,2:T(1,128)}), f32[1,3,32,512]{3,0,1,2:T(1,128)S(1)}, u32[]{:S(2)}, u32[]{:S(2)}) async-start(f32[1,3,32,512]{3,0,1,2:T(1,128)} %copy.89), calls=%async_computation.2 | async-start | bytes 393216 | tf_op jit(solution)/shard_map/all_to_all | solution.py:103
  84.0 11.1 %all-to-all-start.3 = ((f32[8,1,3,4,512]{4,3,2,1,0:T(4,128)}), f32[8,1,3,4,512]{4,3,2,1,0:T(4,128)S(1)}, u32[]{:S(2)}, u32[]{:S(2)}) async-start(f32[8,1,3,4,512]{4,3,2,1,0:T(4,128)} %constant_dynamic-update-slice_fusion.8), calls=%async_computation.3 | async-start | bytes 393216 | tf_op jit(solution)/shard_map/all_to_all | solution.py:107
